TPU v7x, 32 devices: a whole 2x2x4 slice. The times are simulated.
32 devices in a mesh: dp: 4 (over y, x), space: 8 (over z, core).
Axes of the slice: x: 2, y: 2, z: 4, core: 2. Of those that a mesh axis runs over, the one named last changes fastest.
Arguments:
- signal: bfloat16 [4, 512, 64, 1280], P('dp', None, 'space'), may hold values from -6 to 6
- cotangent: bfloat16 [4, 512, 64, 1280], P('dp', None, 'space'), may hold values from -6 to 6
- spec_weight: bfloat16 [2, 20, 20, 73728], P(None, None, None, 'space'), may hold values from -1.25 to 1.25
- point_weight: bfloat16 [20, 20], replicated, may hold values from -1.25 to 1.25
- bias: bfloat16 [20], replicated, may hold values from -3 to 3
Outputs:
- grad_signal: bfloat16 [4, 512, 64, 1280], P('dp', None, 'space')
- spec_grad: float32 [2, 20, 20, 73728], P(None, None, None, ('space', 'dp'))
All inputs are finite; a program needn't handle non-finite values.
Results may differ from a plain program's by a relative error of at most 0.024.
Values may be sent and summed in bfloat16 or wider, within the bound.
No kernel may reach another device: no remote copies, remote signals or barrier semaphores. Data moves between devices by JAX's collectives and lax.ppermute only.
A program may use at most 256 MiB of HBM per device.

v0:
```python
import math
import jax
import jax.numpy as jnp
import ml_dtypes
import numpy as np
from jax import lax
from jax.sharding import PartitionSpec as P

NX = 64
NY = 64
NZ = 32
NT = 16
C = 20
MX = 24
MY = 24
MZ = 16
MT = 8
MZT = 128
BF = ml_dtypes.bfloat16


def retained(mode_count, length):
    positions = np.arange(mode_count)
    return np.where(positions < mode_count // 2, positions, length - mode_count + positions)


def complex_table(mode_count, length):
    freqs = retained(mode_count, length)
    turns = freqs[:, None] * np.arange(length)[None, :] % length
    angles = turns * (2.0 * math.pi / length)
    norm_scale = 1.0 / math.sqrt(length)
    cos_part = np.cos(angles) * norm_scale
    sin_part = np.sin(angles) * norm_scale
    upper_rows = np.stack([cos_part, sin_part], axis=1)
    lower_rows = np.stack([-sin_part, cos_part], axis=1)
    return np.stack([upper_rows, lower_rows], axis=0)


def depth_tables():
    depth_freq = retained(MZ, NZ)
    time_freq = np.arange(MT)
    depth_turns = depth_freq[:, None] * np.arange(NZ)[None, :] % NZ
    time_turns = time_freq[:, None] * np.arange(NT)[None, :] % NT
    turns = depth_turns[:, None, :, None] * NT + time_turns[None, :, None, :] * NZ
    angles = turns * (2.0 * math.pi / (NZ * NT))
    norm_scale = 1.0 / math.sqrt(NZ * NT)
    forward = np.stack([np.cos(angles), -np.sin(angles)], axis=2) * norm_scale
    doubling = np.where(time_freq == 0, 1.0, 2.0)
    inverse = forward * doubling[None, :, None, None, None]
    return (
        forward.reshape(MZT, 2, NZ * NT).astype(BF),
        inverse.reshape(MZT, 2, NZ * NT).astype(BF),
    )


def gelu_slope(pre_act):
    cumulative = 0.5 * (1.0 + lax.erf(pre_act * (1.0 / math.sqrt(2.0))))
    density = jnp.exp(-0.5 * pre_act * pre_act) * (1.0 / math.sqrt(2.0 * math.pi))
    return cumulative + pre_act * density


def block_table(table_y):
    blocks = np.einsum("cd,PjpY->pcYPdj", np.eye(C), table_y)
    return blocks.reshape(2, C * NY, 2 * C * MY).astype(BF)


def dot32(form, left, right):
    return jnp.einsum(form, left, right, preferred_element_type=jnp.float32)


def local(signal, cotangent, spec_weight, point_weight, bias):
    samples, depth_len, x_rows, merged = signal.shape
    depth_np, inverse_np = depth_tables()
    table_y = complex_table(MY, NY)
    table_x = jnp.asarray(complex_table(MX, NX).astype(BF))
    blocks = jnp.asarray(block_table(table_y))
    depth_table = jnp.asarray(depth_np)
    depth_inverse = jnp.asarray(inverse_np)
    point_block = (
        jnp.einsum("co,yz->cyoz", point_weight.astype(jnp.float32), jnp.eye(NY, dtype=jnp.float32))
        .reshape(C * NY, C * NY)
        .astype(jnp.bfloat16)
    )
    bias_row = jnp.repeat(bias.astype(jnp.float32), NY)
    w_real = spec_weight[0]
    w_imag = spec_weight[1]

    def analyse(table, grid_values):
        real = dot32("mz,szxr->smxr", table[:, 0], grid_values).astype(jnp.bfloat16)
        imag = dot32("mz,szxr->smxr", table[:, 1], grid_values).astype(jnp.bfloat16)
        both = dot32("smxr,rK->smxK", real, blocks[0]) + dot32("smxr,rK->smxK", imag, blocks[1])
        both = both.astype(jnp.bfloat16)
        moved = lax.all_to_all(both, "space", split_axis=1, concat_axis=2, tiled=True)
        halves = moved.reshape(samples, moved.shape[1], NX, 2, C * MY)
        total = dot32("Pipx,smxpr->sPmir", table_x, halves).astype(jnp.bfloat16)
        total = total.reshape(samples, 2, -1, MX, C, MY)
        return jnp.transpose(total, (0, 1, 4, 2, 3, 5)).reshape(samples, 2, C, -1)

    def synthesise(table, spectrum):
        unmerged = spectrum.reshape(samples, 2, C, -1, MX, MY)
        moved = jnp.transpose(unmerged, (0, 1, 3, 4, 2, 5)).reshape(samples, 2, -1, MX, C * MY)
        cells = dot32("Pipx,sPmir->smxpr", table_x, moved).astype(jnp.bfloat16)
        cells = cells.reshape(samples, cells.shape[1], NX, 2 * C * MY)
        back = lax.all_to_all(cells, "space", split_axis=2, concat_axis=1, tiled=True)
        real = dot32("smxK,rK->smxr", back, blocks[0]).astype(jnp.bfloat16)
        imag = dot32("smxK,rK->smxr", back, blocks[1]).astype(jnp.bfloat16)
        return dot32("mz,smxr->szxr", table[:, 0], real) + dot32("mz,smxr->szxr", table[:, 1], imag)

    direct = dot32("szxr,rR->szxR", signal, point_block)
    u_hat = analyse(depth_table, signal)
    v_real = dot32("sik,iok->sok", u_hat[:, 0], w_real) - dot32("sik,iok->sok", u_hat[:, 1], w_imag)
    v_imag = dot32("sik,iok->sok", u_hat[:, 1], w_real) + dot32("sik,iok->sok", u_hat[:, 0], w_imag)
    v_hat = jnp.stack([v_real, v_imag], axis=1).astype(jnp.bfloat16)
    pre_act = synthesise(depth_inverse, v_hat) + direct + bias_row
    hidden = (cotangent.astype(jnp.float32) * gelu_slope(pre_act)).astype(jnp.bfloat16)
    h_hat = analyse(depth_inverse, hidden)
    d_real = dot32("sok,iok->sik", h_hat[:, 0], w_real) + dot32("sok,iok->sik", h_hat[:, 1], w_imag)
    d_imag = dot32("sok,iok->sik", h_hat[:, 1], w_real) - dot32("sok,iok->sik", h_hat[:, 0], w_imag)
    d_hat = jnp.stack([d_real, d_imag], axis=1).astype(jnp.bfloat16)
    pointwise = dot32("szxR,rR->szxr", hidden, point_block)
    grad_signal = (synthesise(depth_table, d_hat) + pointwise).astype(jnp.bfloat16)
    u_all = lax.all_to_all(u_hat, "dp", split_axis=3, concat_axis=0, tiled=True)
    h_all = lax.all_to_all(h_hat, "dp", split_axis=3, concat_axis=0, tiled=True)
    u_all = u_all.astype(jnp.float32)
    h_all = h_all.astype(jnp.float32)

    def outer(left, right):
        return jnp.sum(left[:, :, None, :] * right[:, None, :, :], axis=0)

    grad_real = outer(u_all[:, 0], h_all[:, 0]) + outer(u_all[:, 1], h_all[:, 1])
    grad_imag = outer(u_all[:, 0], h_all[:, 1]) - outer(u_all[:, 1], h_all[:, 0])
    return (grad_signal, jnp.stack([grad_real, grad_imag], axis=0))


def solution(mesh):
    return jax.shard_map(
        local,
        mesh=mesh,
        in_specs=(
            P("dp", None, "space", None),
            P("dp", None, "space", None),
            P(None, None, None, "space"),
            P(),
            P(),
        ),
        out_specs=(P("dp", None, "space", None), P(None, None, None, ("space", "dp"))),
        check_vma=False,
    )
```

profile of v0, /device:TPU:0, one launch (start us, length us, event | category | flops | bytes accessed | tf_op | source)
XLA Modules:
  0.0 657.1 jit_solution(13614879044189403960)
XLA Ops:
  0.7 13.3 %fusion.42 = f32[128,8,960]{0,2,1:T(8,128)} fusion(bf16[1280,960,1]{0,1,2:T(8,128)(2,1)} %constant.47, bf16[128,512,1]{1,0,2:T(8,128)(2,1)} %constant.46, bf16[512,8,1280]{2,1,0:T(8,128)(2,1)} %bitcast.305), kind=kOutput, calls=%fused_computation.68 | convolution fusion | flops 3860070400 | bytes 17006592 | tf_op jit(solution)/shard_map/smxr,rK->smxK/dot_general | solution.py:68
  14.0 12.9 %fusion.39 = bf16[1,128,8,960]{1,3,2,0:T(8,128)(2,1)} fusion(f32[128,8,960]{0,2,1:T(8,128)} %fusion.42, bf16[1280,960,1]{0,1,2:T(8,128)(2,1)S(1)} %copy-done.2, bf16[128,512,1]{1,0,2:T(8,128)(2,1)S(1)} %copy-done.5, bf16[512,8,1280]{2,1,0:T(8,128)(2,1)} %bitcast.306), kind=kOutput, calls=%fused_computation.66 | convolution fusion | flops 3862036480 | bytes 18972672 | tf_op jit(solution)/shard_map/smxr,rK->smxK/dot_general | solution.py:68
  31.0 6.5 all-to-all-start
  37.5 29.8 %fusion.66 = (bf16[1,20,20,9216]{3,0,2,1:T(2,128)(2,1)}, bf16[1,20,20,9216]{3,0,2,1:T(2,128)(2,1)}) fusion(bf16[2,20,20,9216]{3,0,2,1:T(2,128)(2,1)} %param.11), kind=kLoop, calls=%fused_computation.96 | loop fusion | bytes 29491200 | tf_op jit(solution)/shard_map/slice | solution.py:86
  67.4 19.2 %all-to-all-done = bf16[1,128,8,960]{3,2,0,1:T(8,128)(2,1)S(1)} async-done(((bf16[1,128,8,960]{3,2,0,1:T(8,128)(2,1)}), bf16[1,128,8,960]{3,2,0,1:T(8,128)(2,1)S(1)}, u32[]{:S(2)}, u32[]{:S(2)}) %all-to-all-start) | async-done | bytes 1966112 | tf_op jit(solution)/shard_map/all_to_all | solution.py:93
  110.0 7.8 %copy.295 = bf16[1,2,20,9216]{2,1,0,3:T(2,128)(2,1)} copy(bf16[1,2,20,9216]{3,1,2,0:T(2,128)(2,1)S(1)} %reshape.297) | data formatting | bytes 1474560 | tf_op jit(solution)/shard_map/reshape | solution.py:97
  117.8 11.3 %reshape.360 = bf16[4,2,46080]{2,1,0:T(2,128)(2,1)} reshape(bf16[9216,1,2,20]{3,2,1,0:T(2,128)(2,1)} %bitcast.294) | data formatting | bytes 1474560
  133.3 19.1 %fusion.8 = (f32[9216,20]{0,1:T(8,128)S(1)}, f32[9216,20]{0,1:T(8,128)S(1)}, f32[9216,20]{0,1:T(8,128)S(1)}, f32[9216,20]{0,1:T(8,128)S(1)}) fusion(f32[9216,20]{0,1:T(8,128)S(1)} %get-tuple-element.43, bf16[1,20,20,9216]{3,0,2,1:T(2,128)(2,1)} %get-tuple-element.33, f32[9216,20]{0,1:T(8,128)S(1)} %get-tuple-element.42, ...), kind=kLoop, calls=%fused_computation.19 | loop fusion | flops 36126720 | bytes 19169280 | tf_op jit(solution)/shard_map/sik,iok->sok/dot_general | solution.py:68
  164.3 6.4 copy.368
  191.8 10.0 %reshape.352 = bf16[1280,1280,1]{1,0,2:T(8,128)(2,1)} reshape(bf16[20,64,20,64]{3,2,1,0:T(8,128)(2,1)} %fusion.23) | data formatting | bytes 6553600 | tf_op jit(solution)/shard_map/convert_element_type | solution.py:82
  201.8 8.6 %convert_element_type.187 = bf16[1280,1280]{1,0:T(8,128)(2,1)S(1)} reshape(bf16[20,64,20,64]{3,2,1,0:T(8,128)(2,1)} %fusion.23) | data formatting | bytes 6553600 | tf_op jit(solution)/shard_map/convert_element_type | solution.py:82
  210.4 16.4 %copy.254 = bf16[1,512,8,1280]{1,3,2,0:T(8,128)(2,1)} copy(bf16[1,512,8,1280]{3,2,1,0:T(8,128)(2,1)} %param.10) | data formatting | bytes 20971520 | tf_op args[1]
  227.0 20.6 %fusion.17 = f32[1280,512,8]{1,0,2:T(8,128)} fusion(bf16[512,8,1280]{2,1,0:T(8,128)(2,1)} %bitcast.307, bf16[1280,1280]{1,0:T(8,128)(2,1)S(1)} %convert_element_type.187), kind=kOutput, calls=%fused_computation.34 | convolution fusion | flops 13421772800 | bytes 34734080 | tf_op jit(solution)/shard_map/szxr,rR->szxR/dot_general | solution.py:68
  247.5 14.2 %reshape.361 = bf16[9216,1,2,20]{3,2,1,0:T(2,128)(2,1)} reshape(bf16[4,2,46080]{2,1,0:T(2,128)(2,1)} %copy-done.3) | data formatting | bytes 1474560
  261.7 10.4 %copy.296 = bf16[1,2,20,9216]{3,1,2,0:T(2,128)(2,1)S(1)} copy(bf16[1,2,20,9216]{2,1,0,3:T(2,128)(2,1)} %bitcast.295) | data formatting | bytes 1474560 | tf_op jit(solution)/shard_map/all_to_all | solution.py:122
  282.4 11.6 %fusion.33 = f32[8,1280,512]{2,1,0:T(8,128)} fusion(bf16[128,512,1]{1,0,2:T(8,128)(2,1)S(1)} %copy-done.8, bf16[128,8,960]{0,2,1:T(8,128)(2,1)} %copy.270, bf16[1280,960,1]{0,1,2:T(8,128)(2,1)S(1)} %copy-done.1), kind=kOutput, calls=%fused_computation.60 | convolution fusion | flops 3860070400 | bytes 25526272 | tf_op jit(solution)/shard_map/mz,smxr->szxr/dot_general | solution.py:68
  293.9 28.3 %fusion.16 = bf16[512,8,1280]{0,2,1:T(8,128)(2,1)} fusion(f32[1280,512,8]{1,0,2:T(8,128)} %fusion.17, f32[8,1280,512]{2,1,0:T(8,128)} %fusion.33, bf16[128,512,1]{1,0,2:T(8,128)(2,1)S(1)} %copy-done.15, bf16[1,512,8,1280]{1,3,2,0:T(8,128)(2,1)} %copy.254, f32[1280]{0:T(1024)S(1)} %add.90, bf16[128,8,960]{0,2,1:T(8,128)(2,1)} %copy.270, ...), kind=kOutput, calls=%fused_computation.32 | convolution fusion | flops 3933470720 | bytes 67474432 | tf_op jit(solution)/shard_map/mz,smxr->szxr/dot_general | solution.py:68
  322.3 12.8 %fusion.58 = f32[128,8,960]{0,2,1:T(8,128)} fusion(bf16[1280,960,1]{0,1,2:T(8,128)(2,1)S(1)} %copy-done.1, bf16[512,8,1280]{0,2,1:T(8,128)(2,1)} %fusion.16, bf16[128,512,1]{1,0,2:T(8,128)(2,1)S(1)} %copy-done.8), kind=kOutput, calls=%fused_computation.79 | convolution fusion | flops 3860070400 | bytes 17006592 | tf_op jit(solution)/shard_map/smxr,rK->smxK/dot_general | solution.py:68
  335.0 12.9 %fusion.40 = bf16[1,128,8,960]{1,3,2,0:T(8,128)(2,1)S(1)} fusion(f32[128,8,960]{0,2,1:T(8,128)} %fusion.58, bf16[1280,960,1]{0,1,2:T(8,128)(2,1)} %constant.49, bf16[512,8,1280]{0,2,1:T(8,128)(2,1)} %fusion.16, bf16[128,512,1]{1,0,2:T(8,128)(2,1)S(1)} %copy-done.15), kind=kOutput, calls=%fused_computation.67 | convolution fusion | flops 3862036480 | bytes 18972672 | tf_op jit(solution)/shard_map/smxr,rK->smxK/dot_general | solution.py:68
  358.7 21.4 %fusion.69 = f32[512,8,1280]{0,2,1:T(8,128)} fusion(bf16[1280,1280,1]{1,0,2:T(8,128)(2,1)} %reshape.352, bf16[512,8,1280]{0,2,1:T(8,128)(2,1)} %fusion.16), kind=kOutput, calls=%fused_computation.99 | convolution fusion | flops 13421772800 | bytes 34734080 | tf_op jit(solution)/shard_map/szxR,rR->szxr/dot_general | solution.py:68
  380.1 25.0 %all-to-all-done.2 = bf16[1,128,8,960]{3,2,0,1:T(8,128)(2,1)S(1)} async-done(((bf16[1,128,8,960]{3,2,0,1:T(8,128)(2,1)}), bf16[1,128,8,960]{3,2,0,1:T(8,128)(2,1)S(1)}, u32[]{:S(2)}, u32[]{:S(2)}) %all-to-all-start.2) | async-done | bytes 1966112 | tf_op jit(solution)/shard_map/all_to_all | solution.py:93
  427.8 7.8 %copy.297 = bf16[1,2,20,9216]{2,1,0,3:T(2,128)(2,1)} copy(bf16[1,2,20,9216]{3,1,2,0:T(2,128)(2,1)S(1)} %reshape.308) | data formatting | bytes 1474560 | tf_op jit(solution)/shard_map/reshape | solution.py:97
  435.9 11.2 %reshape.362 = bf16[4,2,46080]{2,1,0:T(2,128)(2,1)} reshape(bf16[9216,1,2,20]{3,2,1,0:T(2,128)(2,1)} %bitcast.293) | data formatting | bytes 1474560
  451.5 22.1 %fusion.12 = (f32[9216,20]{0,1:T(8,128)S(1)}, f32[9216,20]{0,1:T(8,128)S(1)}, f32[9216,20]{0,1:T(8,128)S(1)}, f32[9216,20]{0,1:T(8,128)S(1)}) fusion(f32[9216,20]{0,1:T(8,128)S(1)} %bitcast_convert_fusion.5, bf16[1,20,20,9216]{3,0,2,1:T(2,128)(2,1)} %get-tuple-element.33, f32[9216,20]{0,1:T(8,128)S(1)} %bitcast_convert_fusion.4, ...), kind=kLoop, calls=%fused_computation.23 | loop fusion | flops 36126720 | bytes 19169280 | tf_op jit(solution)/shard_map/sok,iok->sik/dot_general | solution.py:68
  485.4 6.4 copy.373
  507.8 12.7 %reshape.363 = bf16[9216,1,2,20]{3,2,1,0:T(2,128)(2,1)} reshape(bf16[4,2,46080]{2,1,0:T(2,128)(2,1)S(1)} %all-to-all-done.5) | data formatting | bytes 1474560
  520.5 10.0 %copy.298 = bf16[1,2,20,9216]{3,1,2,0:T(2,128)(2,1)S(1)} copy(bf16[1,2,20,9216]{2,1,0,3:T(2,128)(2,1)} %bitcast.296) | data formatting | bytes 1474560 | tf_op jit(solution)/shard_map/all_to_all | solution.py:123
  532.4 40.5 %multiply_reduce_fusion.2 = (f32[20,20,2304]{2,1,0:T(8,128)S(1)}, f32[20,20,2304]{2,1,0:T(8,128)S(1)}, f32[20,20,2304]{2,1,0:T(8,128)S(1)}, f32[20,20,2304]{2,1,0:T(8,128)S(1)}) fusion(f32[4,20,2304]{2,0,1:T(4,128)} %get-tuple-element.37, f32[4,20,2304]{2,0,1:T(4,128)} %get-tuple-element.35, f32[4,20,2304]{2,0,1:T(4,128)} %get-tuple-element.36, ...), kind=kLoop, calls=%fused_computation.30 | loop fusion | flops 25804800 | bytes 17694720 | tf_op jit(solution)/shard_map/reduce_sum | solution.py:128
  581.9 12.3 %copy.300 = f32[2,20,20,2304]{3,0,2,1:T(2,128)} copy(f32[2,20,20,2304]{3,2,1,0:T(8,128)} %pad_maximum_fusion) | data formatting | bytes 14745600
  601.6 13.3 %fusion.34 = f32[8,1280,512]{2,1,0:T(8,128)} fusion(bf16[128,512,1]{1,0,2:T(8,128)(2,1)S(1)} %copy-done.7, bf16[128,8,960]{0,2,1:T(8,128)(2,1)S(1)} %copy.289, bf16[1280,960,1]{0,1,2:T(8,128)(2,1)} %constant.47), kind=kOutput, calls=%fused_computation.61 | convolution fusion | flops 3860070400 | bytes 25526272 | tf_op jit(solution)/shard_map/mz,smxr->szxr/dot_general | solution.py:68
  615.0 25.0 %fusion.6 = bf16[1,512,8,1280]{1,3,2,0:T(8,128)(2,1)} fusion(f32[512,8,1280]{0,2,1:T(8,128)} %fusion.69, f32[8,1280,512]{2,1,0:T(8,128)} %fusion.34, bf16[128,512,1]{1,0,2:T(8,128)(2,1)S(1)} %copy-done.6, bf16[128,8,960]{0,2,1:T(8,128)(2,1)S(1)} %copy.289, bf16[1280,960,1]{0,1,2:T(8,128)(2,1)} %constant.49), kind=kOutput, calls=%fused_computation.16 | convolution fusion | flops 3875799040 | bytes 56983552 | tf_op jit(solution)/shard_map/mz,smxr->szxr/dot_general | solution.py:68
  640.0 16.6 %copy.299 = bf16[1,512,8,1280]{3,2,1,0:T(8,128)(2,1)} copy(bf16[1,512,8,1280]{1,3,2,0:T(8,128)(2,1)} %fusion.6) | data formatting | bytes 20971520
  (96 shorter events, 159.2 us)
Async XLA Ops:
  0.6 13.3 %copy-start.2 = (bf16[1280,960,1]{0,1,2:T(8,128)(2,1)S(1)}, bf16[1280,960,1]{0,1,2:T(8,128)(2,1)}, u32[]{:S(2)}) copy-start(bf16[1280,960,1]{0,1,2:T(8,128)(2,1)} %constant.49) | copy-start | bytes 7372804
  0.6 13.3 %copy-start.5 = (bf16[128,512,1]{1,0,2:T(8,128)(2,1)S(1)}, bf16[128,512,1]{1,0,2:T(8,128)(2,1)}, u32[]{:S(2)}) copy-start(bf16[128,512,1]{1,0,2:T(8,128)(2,1)} %constant.48) | copy-start | bytes 393220
  31.0 55.6 %all-to-all-start = ((bf16[1,128,8,960]{3,2,0,1:T(8,128)(2,1)}), bf16[1,128,8,960]{3,2,0,1:T(8,128)(2,1)S(1)}, u32[]{:S(2)}, u32[]{:S(2)}) async-start(bf16[1,128,8,960]{3,2,0,1:T(8,128)(2,1)} %copy.257), calls=%async_computation | async-start | bytes 4194304 | tf_op jit(solution)/shard_map/all_to_all | solution.py:93
  37.5 29.8 %copy-start.13 = (bf16[20,20]{1,0:T(8,128)(2,1)S(1)}, bf16[20,20]{1,0:T(8,128)(2,1)}, u32[]{:S(2)}) copy-start(bf16[20,20]{1,0:T(8,128)(2,1)} %param.12) | copy-start | bytes 2404
  67.3 24.4 %copy-start.11 = (bf16[2,24,2,64,1]{3,1,2,0,4:T(8,128)(2,1)S(1)}, bf16[2,24,2,64,1]{3,1,2,0,4:T(8,128)(2,1)}, u32[]{:S(2)}) copy-start(bf16[2,24,2,64,1]{3,1,2,0,4:T(8,128)(2,1)} %constant.50) | copy-start | bytes 36868
  117.8 15.2 %copy-start.4 = (bf16[1,1,20,9216]{3,1,2,0:T(2,128)(2,1)S(1)}, bf16[1,1,20,9216]{3,1,2,0:T(2,128)(2,1)}, u32[]{:S(2)}) copy-start(bf16[1,1,20,9216]{3,1,2,0:T(2,128)(2,1)} %get-tuple-element.41) | copy-start | bytes 1105924
  129.1 53.2 %all-to-all-start.4 = ((bf16[4,2,46080]{2,1,0:T(2,128)(2,1)}), bf16[4,2,46080]{2,1,0:T(2,128)(2,1)S(1)}, u32[]{:S(2)}, u32[]{:S(2)}) async-start(bf16[4,2,46080]{2,1,0:T(2,128)(2,1)} %reshape.360), calls=%async_computation.4 | async-start | bytes 1474560 | tf_op jit(solution)/shard_map/all_to_all | solution.py:122
  170.8 5.6 copy-start.9
  182.3 9.6 %copy-start.3 = (bf16[4,2,46080]{2,1,0:T(2,128)(2,1)}, bf16[4,2,46080]{2,1,0:T(2,128)(2,1)S(1)}, u32[]{:S(2)}) copy-start(bf16[4,2,46080]{2,1,0:T(2,128)(2,1)S(1)} %all-to-all-done.4) | copy-start | bytes 2211844
  182.3 91.6 %all-to-all-start.1 = ((bf16[1,16,64,960]{3,1,0,2:T(8,128)(2,1)}), bf16[1,16,64,960]{3,1,0,2:T(8,128)(2,1)}, u32[]{:S(2)}, u32[]{:S(2)}) async-start(bf16[1,16,64,960]{3,1,0,2:T(8,128)(2,1)} %reshape.355), calls=%async_computation.1 | async-start | bytes 4194304 | tf_op jit(solution)/shard_map/all_to_all | solution.py:104
  210.4 16.4 %copy-start.14 = (bf16[20]{0:T(256)(128)(2,1)S(1)}, bf16[20]{0:T(256)(128)(2,1)}, u32[]{:S(2)}) copy-start(bf16[20]{0:T(256)(128)(2,1)} %param.13) | copy-start | bytes 124
  273.9 8.5 %copy-start.1 = (bf16[1280,960,1]{0,1,2:T(8,128)(2,1)S(1)}, bf16[1280,960,1]{0,1,2:T(8,128)(2,1)}, u32[]{:S(2)}) copy-start(bf16[1280,960,1]{0,1,2:T(8,128)(2,1)} %constant.47) | copy-start | bytes 7372804
  273.9 8.5 %copy-start.8 = (bf16[128,512,1]{1,0,2:T(8,128)(2,1)S(1)}, bf16[128,512,1]{1,0,2:T(8,128)(2,1)}, u32[]{:S(2)}) copy-start(bf16[128,512,1]{1,0,2:T(8,128)(2,1)} %constant.53) | copy-start | bytes 393220
  282.3 11.6 %copy-start.15 = (bf16[128,512,1]{1,0,2:T(8,128)(2,1)S(1)}, bf16[128,512,1]{1,0,2:T(8,128)(2,1)}, u32[]{:S(2)}) copy-start(bf16[128,512,1]{1,0,2:T(8,128)(2,1)} %constant.54) | copy-start | bytes 393220
  350.8 54.3 %all-to-all-start.2 = ((bf16[1,128,8,960]{3,2,0,1:T(8,128)(2,1)}), bf16[1,128,8,960]{3,2,0,1:T(8,128)(2,1)S(1)}, u32[]{:S(2)}, u32[]{:S(2)}) async-start(bf16[1,128,8,960]{3,2,0,1:T(8,128)(2,1)} %copy.278), calls=%async_computation.2 | async-start | bytes 4194304 | tf_op jit(solution)/shard_map/all_to_all | solution.py:93
  380.1 30.2 %copy-start.12 = (bf16[2,24,2,64,1]{3,1,2,0,4:T(8,128)(2,1)S(1)}, bf16[2,24,2,64,1]{3,1,2,0,4:T(8,128)(2,1)}, u32[]{:S(2)}) copy-start(bf16[2,24,2,64,1]{3,1,2,0,4:T(8,128)(2,1)} %constant.50) | copy-start | bytes 36868
  447.1 56.2 %all-to-all-start.5 = ((bf16[4,2,46080]{2,1,0:T(2,128)(2,1)}), bf16[4,2,46080]{2,1,0:T(2,128)(2,1)S(1)}, u32[]{:S(2)}, u32[]{:S(2)}) async-start(bf16[4,2,46080]{2,1,0:T(2,128)(2,1)} %reshape.362), calls=%async_computation.5 | async-start | bytes 1474560 | tf_op jit(solution)/shard_map/all_to_all | solution.py:123
  491.8 5.6 copy-start.10
  503.3 90.8 %all-to-all-start.3 = ((bf16[1,16,64,960]{3,1,0,2:T(8,128)(2,1)}), bf16[1,16,64,960]{3,1,0,2:T(8,128)(2,1)}, u32[]{:S(2)}, u32[]{:S(2)}) async-start(bf16[1,16,64,960]{3,1,0,2:T(8,128)(2,1)} %reshape.358), calls=%async_computation.3 | async-start | bytes 4194304 | tf_op jit(solution)/shard_map/all_to_all | solution.py:104
  575.5 2.3 copy-start
  594.1 7.5 %copy-start.7 = (bf16[128,512,1]{1,0,2:T(8,128)(2,1)S(1)}, bf16[128,512,1]{1,0,2:T(8,128)(2,1)}, u32[]{:S(2)}) copy-start(bf16[128,512,1]{1,0,2:T(8,128)(2,1)} %constant.46) | copy-start | bytes 393220
  601.6 13.3 %copy-start.6 = (bf16[128,512,1]{1,0,2:T(8,128)(2,1)S(1)}, bf16[128,512,1]{1,0,2:T(8,128)(2,1)}, u32[]{:S(2)}) copy-start(bf16[128,512,1]{1,0,2:T(8,128)(2,1)} %constant.48) | copy-start | bytes 393220
where the time goes:
time: 668 us; the launch traced here: 657 us
  local copies, waits for them, and re-layouts  306 us (46%)
  matrix products  175 us (26%)
  other arithmetic  101 us (15%)
  waiting for transfers between devices  44.2 us (7%)
  starting transfers between devices  29.2 us (4%)
    dot_general x14, matrix products, dot32(): return jnp.einsum(form, left, right, preferred_element_type=jnp.float32)  175 us
    unnamed x39, local copies, waits for them, and re-layouts  96.5 us
    all_to_all x2, waiting for transfers between devices, analyse(): lax.all_to_all(both, 'space', split_axis=1, concat_axis=2, tiled=True)  44.2 us
    dot_general x2, other arithmetic, dot32(): return jnp.einsum(form, left, right, preferred_element_type=jnp.float32)  41.2 us
    reduce_sum x1, other arithmetic, outer(): return jnp.sum(left[:, :, None, :] * right[:, None, :, :], axis=0)  40.5 us
    another operation x8, local copies, waits for them, and re-layouts  38.5 us
    slice x1, local copies, waits for them, and re-layouts, local(): w_imag = spec_weight[1]  29.8 us
    reshape x4, local copies, waits for them, and re-layouts, analyse(): return jnp.transpose(total, (0, 1, 4, 2, 3, 5)).reshape(samples, 2, C, -1)  27.9 us
  transfers between devices with their start and end apart: 6, of which 2 were waited for; matrix products, arithmetic and copies ran while one was open for 50% of the time, Pallas kernels for 0%

commit v1 on v0

--- a/solution.py
+++ b/solution.py
@@ -17,6 +17,19 @@
 MT = 8
 MZT = 128
 BF = ml_dtypes.bfloat16
+
+
+def find_ports(raw, axis_no, base_x):
+    block_next, right_arr = (raw.shape[:axis_no], raw.shape[axis_no + 1 :])
+    then = jnp.moveaxis(raw.reshape(*block_next, base_x, -1, *right_arr), axis_no, 0)
+    return then
+
+
+def rows_match(x_part, dim_k):
+    field_out = list(x_part.shape[1:])
+    field_out[dim_k] *= x_part.shape[0]
+    q_next = jnp.moveaxis(x_part, 0, dim_k).reshape(field_out)
+    return q_next
 
 
 def retained(mode_count, length):
@@ -120,7 +133,17 @@
     pointwise = dot32("szxR,rR->szxr", hidden, point_block)
     grad_signal = (synthesise(depth_table, d_hat) + pointwise).astype(jnp.bfloat16)
     u_all = lax.all_to_all(u_hat, "dp", split_axis=3, concat_axis=0, tiled=True)
-    h_all = lax.all_to_all(h_hat, "dp", split_axis=3, concat_axis=0, tiled=True)
+    f_now = lax.axis_size("dp")
+    vec_out = lax.axis_index("dp")
+    spare, p_next = (f_now, vec_out)
+    r_now = find_ports(h_hat, 3, spare)
+    leaves = [r_now[p_next]]
+    for idx in range(1, spare):
+        seen_now = r_now[p_next ^ idx]
+        leaves.append(lax.ppermute(seen_now, "dp", [(j, j ^ idx) for j in range(spare)]))
+    r1 = jnp.stack(leaves, axis=0)
+    r_now = r1[p_next ^ jnp.arange(spare)]
+    h_all = rows_match(r_now, 0)
     u_all = u_all.astype(jnp.float32)
     h_all = h_all.astype(jnp.float32)
 

time: 668 us -> 643 us (0.963)
  local copies, waits for them, and re-layouts: 306 us -> 280 us
    unnamed x39 -> x43, local copies, waits for them, and re-layouts: 96.5 us -> 72.6 us
    another operation x8 -> x14, local copies, waits for them, and re-layouts: 38.5 us -> 48.6 us
    all_to_all x1 -> x0, local copies, waits for them, and re-layouts: 9.98 us -> none  [local(): h_all = lax.all_to_all(h_hat, 'dp', split_axis=3, concat_axis=0, tiled=True)]
    reshape x4 -> x3, local copies, waits for them, and re-layouts: 27.9 us -> 20.1 us  [analyse(): return jnp.transpose(total, (0, 1, 4, 2, 3, 5)).reshape(samples, 2, C, -1)]
    transpose x2 -> x3, local copies, waits for them, and re-layouts: 10.4 us -> 13.4 us  [analyse(): return jnp.transpose(total, (0, 1, 4, 2, 3, 5)).reshape(samples, 2, C, -1)]
  transfers between devices with their start and end apart: 6 -> 8, of which waited for: 2 -> 2; matrix products, arithmetic and copies ran while one was open for 50% -> 44% of each run, Pallas kernels for 0% -> 0%
where the time goes in v1:
time: 643 us; the launch traced here: 632 us
  local copies, waits for them, and re-layouts  280 us (44%)
  matrix products  175 us (27%)
  other arithmetic  103 us (16%)
  waiting for transfers between devices  44.2 us (7%)
  starting transfers between devices  28.3 us (4%)
    dot_general x14, matrix products, dot32(): return jnp.einsum(form, left, right, preferred_element_type=jnp.float32)  175 us
    unnamed x43, local copies, waits for them, and re-layouts  72.6 us
    all_to_all x2, waiting for transfers between devices, analyse(): lax.all_to_all(both, 'space', split_axis=1, concat_axis=2, tiled=True)  44.2 us
    dot_general x2, other arithmetic, dot32(): return jnp.einsum(form, left, right, preferred_element_type=jnp.float32)  42.3 us
    another operation x13, local copies, waits for them, and re-layouts  41.7 us
    reduce_sum x1, other arithmetic, outer(): return jnp.sum(left[:, :, None, :] * right[:, None, :, :], axis=0)  40.5 us
    slice x1, local copies, waits for them, and re-layouts, local(): w_imag = spec_weight[1]  29.8 us
    reshape x3, local copies, waits for them, and re-layouts, analyse(): return jnp.transpose(total, (0, 1, 4, 2, 3, 5)).reshape(samples, 2, C, -1)  20.1 us
  transfers between devices with their start and end apart: 8, of which 2 were waited for; matrix products, arithmetic and copies ran while one was open for 44% of the time, Pallas kernels for 0%

profile of v1, /device:TPU:0, one launch (start us, length us, event | category | flops | bytes accessed | tf_op | source)
XLA Modules:
  0.0 632.4 jit_solution(6309069969381444963)
XLA Ops:
  0.7 13.3 %fusion.42 = f32[128,8,960]{0,2,1:T(8,128)} fusion(bf16[1280,960,1]{0,1,2:T(8,128)(2,1)} %constant.64, bf16[128,512,1]{1,0,2:T(8,128)(2,1)} %constant.63, bf16[512,8,1280]{2,1,0:T(8,128)(2,1)} %bitcast.331), kind=kOutput, calls=%fused_computation.69 | convolution fusion | flops 3860070400 | bytes 17006592 | tf_op jit(solution)/shard_map/smxr,rK->smxK/dot_general | solution.py:81
  14.0 12.9 %fusion.39 = bf16[1,128,8,960]{1,3,2,0:T(8,128)(2,1)} fusion(f32[128,8,960]{0,2,1:T(8,128)} %fusion.42, bf16[1280,960,1]{0,1,2:T(8,128)(2,1)S(1)} %copy-done.2, bf16[128,512,1]{1,0,2:T(8,128)(2,1)S(1)} %copy-done.6, bf16[512,8,1280]{2,1,0:T(8,128)(2,1)} %bitcast.332), kind=kOutput, calls=%fused_computation.67 | convolution fusion | flops 3862036480 | bytes 18972672 | tf_op jit(solution)/shard_map/smxr,rK->smxK/dot_general | solution.py:81
  31.0 6.6 %all-to-all-start = ((bf16[1,128,8,960]{3,2,0,1:T(8,128)(2,1)}), bf16[1,128,8,960]{3,2,0,1:T(8,128)(2,1)S(1)}, u32[]{:S(2)}, u32[]{:S(2)}) async-start(bf16[1,128,8,960]{3,2,0,1:T(8,128)(2,1)} %copy.285), calls=%async_computation | async-start | bytes 4194304 | tf_op jit(solution)/shard_map/all_to_all | solution.py:106
  37.6 29.8 %fusion.67 = (bf16[1,20,20,9216]{3,0,2,1:T(2,128)(2,1)}, bf16[1,20,20,9216]{3,0,2,1:T(2,128)(2,1)}) fusion(bf16[2,20,20,9216]{3,0,2,1:T(2,128)(2,1)} %param.11), kind=kLoop, calls=%fused_computation.109 | loop fusion | bytes 29491200 | tf_op jit(solution)/shard_map/slice | solution.py:99
  67.4 19.1 %all-to-all-done = bf16[1,128,8,960]{3,2,0,1:T(8,128)(2,1)S(1)} async-done(((bf16[1,128,8,960]{3,2,0,1:T(8,128)(2,1)}), bf16[1,128,8,960]{3,2,0,1:T(8,128)(2,1)S(1)}, u32[]{:S(2)}, u32[]{:S(2)}) %all-to-all-start) | async-done | bytes 1966112 | tf_op jit(solution)/shard_map/all_to_all | solution.py:106
  102.0 6.2 reshape.319
  110.1 7.8 %copy.323 = bf16[1,2,20,9216]{2,1,0,3:T(2,128)(2,1)} copy(bf16[1,2,20,9216]{3,1,2,0:T(2,128)(2,1)S(1)} %reshape.319) | data formatting | bytes 1474560 | tf_op jit(solution)/shard_map/reshape | solution.py:110
  117.9 11.2 %reshape.393 = bf16[4,2,46080]{2,1,0:T(2,128)(2,1)} reshape(bf16[9216,1,2,20]{3,2,1,0:T(2,128)(2,1)} %bitcast.314) | data formatting | bytes 1474560
  133.5 19.1 %fusion.8 = (f32[9216,20]{0,1:T(8,128)S(1)}, f32[9216,20]{0,1:T(8,128)S(1)}, f32[9216,20]{0,1:T(8,128)S(1)}, f32[9216,20]{0,1:T(8,128)S(1)}) fusion(f32[9216,20]{0,1:T(8,128)S(1)} %get-tuple-element.47, bf16[1,20,20,9216]{3,0,2,1:T(2,128)(2,1)} %get-tuple-element.33, f32[9216,20]{0,1:T(8,128)S(1)} %get-tuple-element.46, ...), kind=kLoop, calls=%fused_computation.20 | loop fusion | flops 36126720 | bytes 19169280 | tf_op jit(solution)/shard_map/sik,iok->sok/dot_general | solution.py:81
  164.3 6.4 %copy.402 = bf16[1,2,16,24,20,24]{5,4,3,1,2,0:T(8,128)(2,1)} copy(bf16[1,2,16,24,20,24]{5,3,2,4,1,0:T(8,128)(2,1)S(1)} %maximum_bitcast_fusion) | data formatting | bytes 1474560 | tf_op jit(solution)/shard_map/reshape.35
  191.8 10.0 %reshape.385 = bf16[1280,1280,1]{1,0,2:T(8,128)(2,1)} reshape(bf16[20,64,20,64]{3,2,1,0:T(8,128)(2,1)} %fusion.23) | data formatting | bytes 6553600 | tf_op jit(solution)/shard_map/convert_element_type | solution.py:95
  201.7 8.6 %convert_element_type.181 = bf16[1280,1280]{1,0:T(8,128)(2,1)S(1)} reshape(bf16[20,64,20,64]{3,2,1,0:T(8,128)(2,1)} %fusion.23) | data formatting | bytes 6553600 | tf_op jit(solution)/shard_map/convert_element_type | solution.py:95
  210.4 16.4 %copy.282 = bf16[1,512,8,1280]{1,3,2,0:T(8,128)(2,1)} copy(bf16[1,512,8,1280]{3,2,1,0:T(8,128)(2,1)} %param.10) | data formatting | bytes 20971520 | tf_op args[1]
  227.5 20.6 %fusion.17 = f32[1280,512,8]{1,0,2:T(8,128)} fusion(bf16[512,8,1280]{2,1,0:T(8,128)(2,1)} %bitcast.333, bf16[1280,1280]{1,0:T(8,128)(2,1)S(1)} %convert_element_type.181), kind=kOutput, calls=%fused_computation.35 | convolution fusion | flops 13421772800 | bytes 34734080 | tf_op jit(solution)/shard_map/szxr,rR->szxR/dot_general | solution.py:81
  248.2 14.2 %reshape.394 = bf16[9216,1,2,20]{3,2,1,0:T(2,128)(2,1)} reshape(bf16[4,2,46080]{2,1,0:T(2,128)(2,1)} %copy-done.4) | data formatting | bytes 1474560
  262.4 10.4 %copy.324 = bf16[1,2,20,9216]{3,1,2,0:T(2,128)(2,1)S(1)} copy(bf16[1,2,20,9216]{2,1,0,3:T(2,128)(2,1)} %bitcast.315) | data formatting | bytes 1474560 | tf_op jit(solution)/shard_map/all_to_all | solution.py:135
  283.0 11.6 %fusion.33 = f32[8,1280,512]{2,1,0:T(8,128)} fusion(bf16[128,512,1]{1,0,2:T(8,128)(2,1)S(1)} %copy-done.9, bf16[128,8,960]{0,2,1:T(8,128)(2,1)} %copy.298, bf16[1280,960,1]{0,1,2:T(8,128)(2,1)S(1)} %copy-done.1), kind=kOutput, calls=%fused_computation.61 | convolution fusion | flops 3860070400 | bytes 25526272 | tf_op jit(solution)/shard_map/mz,smxr->szxr/dot_general | solution.py:81
  294.6 28.3 %fusion.16 = bf16[512,8,1280]{0,2,1:T(8,128)(2,1)} fusion(f32[1280,512,8]{1,0,2:T(8,128)} %fusion.17, f32[8,1280,512]{2,1,0:T(8,128)} %fusion.33, bf16[128,512,1]{1,0,2:T(8,128)(2,1)S(1)} %copy-done.16, bf16[1,512,8,1280]{1,3,2,0:T(8,128)(2,1)} %copy.282, f32[1280]{0:T(1024)S(1)} %add.112, bf16[128,8,960]{0,2,1:T(8,128)(2,1)} %copy.298, ...), kind=kOutput, calls=%fused_computation.33 | convolution fusion | flops 3933470720 | bytes 67474432 | tf_op jit(solution)/shard_map/mz,smxr->szxr/dot_general | solution.py:81
  323.0 12.8 %fusion.58 = f32[128,8,960]{0,2,1:T(8,128)} fusion(bf16[1280,960,1]{0,1,2:T(8,128)(2,1)S(1)} %copy-done.1, bf16[512,8,1280]{0,2,1:T(8,128)(2,1)} %fusion.16, bf16[128,512,1]{1,0,2:T(8,128)(2,1)S(1)} %copy-done.9), kind=kOutput, calls=%fused_computation.80 | convolution fusion | flops 3860070400 | bytes 17006592 | tf_op jit(solution)/shard_map/smxr,rK->smxK/dot_general | solution.py:81
  335.7 13.0 %fusion.40 = bf16[1,128,8,960]{1,3,2,0:T(8,128)(2,1)S(1)} fusion(f32[128,8,960]{0,2,1:T(8,128)} %fusion.58, bf16[1280,960,1]{0,1,2:T(8,128)(2,1)} %constant.66, bf16[512,8,1280]{0,2,1:T(8,128)(2,1)} %fusion.16, bf16[128,512,1]{1,0,2:T(8,128)(2,1)S(1)} %copy-done.16), kind=kOutput, calls=%fused_computation.68 | convolution fusion | flops 3862036480 | bytes 18972672 | tf_op jit(solution)/shard_map/smxr,rK->smxK/dot_general | solution.py:81
  359.3 21.5 %fusion.71 = f32[512,8,1280]{0,2,1:T(8,128)} fusion(bf16[1280,1280,1]{1,0,2:T(8,128)(2,1)} %reshape.385, bf16[512,8,1280]{0,2,1:T(8,128)(2,1)} %fusion.16), kind=kOutput, calls=%fused_computation.113 | convolution fusion | flops 13421772800 | bytes 34734080 | tf_op jit(solution)/shard_map/szxR,rR->szxr/dot_general | solution.py:81
  380.8 25.0 %all-to-all-done.2 = bf16[1,128,8,960]{3,2,0,1:T(8,128)(2,1)S(1)} async-done(((bf16[1,128,8,960]{3,2,0,1:T(8,128)(2,1)}), bf16[1,128,8,960]{3,2,0,1:T(8,128)(2,1)S(1)}, u32[]{:S(2)}, u32[]{:S(2)}) %all-to-all-start.2) | async-done | bytes 1966112 | tf_op jit(solution)/shard_map/all_to_all | solution.py:106
  424.3 6.2 reshape.330
  431.8 23.1 %fusion.12 = (f32[9216,20]{0,1:T(8,128)S(1)}, f32[9216,20]{0,1:T(8,128)S(1)}, f32[9216,20]{0,1:T(8,128)S(1)}, f32[9216,20]{0,1:T(8,128)}) fusion(f32[9216,20]{0,1:T(8,128)S(1)} %bitcast_convert_fusion.5, bf16[1,20,20,9216]{3,0,2,1:T(2,128)(2,1)} %get-tuple-element.33, f32[9216,20]{0,1:T(8,128)S(1)} %bitcast_convert_fusion.4, ...), kind=kLoop, calls=%fused_computation.24 | loop fusion | flops 36126720 | bytes 19169280 | tf_op jit(solution)/shard_map/sok,iok->sik/dot_general | solution.py:81
  463.8 7.0 %reshape_reshape.3 = bf16[1,2,20,4,2304]{4,3,2,1,0:T(4,128)(2,1)S(1)} reshape(bf16[1,2,20,16,24,24]{5,4,3,2,1,0:T(8,128)(2,1)} %copy.325) | data formatting | bytes 1474560 | tf_op jit(solution)/shard_map/reshape;reshape | solution.py:24
  478.2 6.4 %copy.407 = bf16[1,2,16,24,20,24]{5,4,3,1,2,0:T(8,128)(2,1)} copy(bf16[1,2,16,24,20,24]{5,3,2,4,1,0:T(8,128)(2,1)S(1)} %maximum_bitcast_fusion.1) | data formatting | bytes 1474560 | tf_op jit(solution)/shard_map/reshape.67
  484.6 5.7 reshape.382
  507.6 40.5 %multiply_reduce_fusion.2 = (f32[20,20,2304]{2,1,0:T(8,128)S(1)}, f32[20,20,2304]{2,1,0:T(8,128)S(1)}, f32[20,20,2304]{2,1,0:T(8,128)S(1)}, f32[20,20,2304]{2,1,0:T(8,128)S(1)}) fusion(f32[4,20,2304]{2,0,1:T(4,128)} %bitcast.323, f32[4,20,2304]{2,0,1:T(4,128)} %get-tuple-element.35, f32[4,20,2304]{2,0,1:T(4,128)} %bitcast.324, ...), kind=kLoop, calls=%fused_computation.31 | loop fusion | flops 25804800 | bytes 17694720 | tf_op jit(solution)/shard_map/reduce_sum | solution.py:151
  557.1 12.3 %copy.334 = f32[2,20,20,2304]{3,0,2,1:T(2,128)} copy(f32[2,20,20,2304]{3,2,1,0:T(8,128)} %pad_maximum_fusion) | data formatting | bytes 14745600
  576.9 13.4 %fusion.34 = f32[8,1280,512]{2,1,0:T(8,128)} fusion(bf16[128,512,1]{1,0,2:T(8,128)(2,1)S(1)} %copy-done.8, bf16[128,8,960]{0,2,1:T(8,128)(2,1)S(1)} %copy.317, bf16[1280,960,1]{0,1,2:T(8,128)(2,1)} %constant.64), kind=kOutput, calls=%fused_computation.62 | convolution fusion | flops 3860070400 | bytes 25526272 | tf_op jit(solution)/shard_map/mz,smxr->szxr/dot_general | solution.py:81
  590.3 25.0 %fusion.6 = bf16[1,512,8,1280]{1,3,2,0:T(8,128)(2,1)} fusion(f32[512,8,1280]{0,2,1:T(8,128)} %fusion.71, f32[8,1280,512]{2,1,0:T(8,128)} %fusion.34, bf16[128,512,1]{1,0,2:T(8,128)(2,1)S(1)} %copy-done.7, bf16[128,8,960]{0,2,1:T(8,128)(2,1)S(1)} %copy.317, bf16[1280,960,1]{0,1,2:T(8,128)(2,1)} %constant.66), kind=kOutput, calls=%fused_computation.17 | convolution fusion | flops 3875799040 | bytes 56983552 | tf_op jit(solution)/shard_map/mz,smxr->szxr/dot_general | solution.py:81
  615.3 16.6 %copy.333 = bf16[1,512,8,1280]{3,2,1,0:T(8,128)(2,1)} copy(bf16[1,512,8,1280]{1,3,2,0:T(8,128)(2,1)} %fusion.6) | data formatting | bytes 20971520
  (115 shorter events, 149.6 us)
Async XLA Ops:
  0.6 13.3 %copy-start.2 = (bf16[1280,960,1]{0,1,2:T(8,128)(2,1)S(1)}, bf16[1280,960,1]{0,1,2:T(8,128)(2,1)}, u32[]{:S(2)}) copy-start(bf16[1280,960,1]{0,1,2:T(8,128)(2,1)} %constant.66) | copy-start | bytes 7372804
  0.6 13.3 %copy-start.6 = (bf16[128,512,1]{1,0,2:T(8,128)(2,1)S(1)}, bf16[128,512,1]{1,0,2:T(8,128)(2,1)}, u32[]{:S(2)}) copy-start(bf16[128,512,1]{1,0,2:T(8,128)(2,1)} %constant.65) | copy-start | bytes 393220
  31.0 55.6 %all-to-all-start = ((bf16[1,128,8,960]{3,2,0,1:T(8,128)(2,1)}), bf16[1,128,8,960]{3,2,0,1:T(8,128)(2,1)S(1)}, u32[]{:S(2)}, u32[]{:S(2)}) async-start(bf16[1,128,8,960]{3,2,0,1:T(8,128)(2,1)} %copy.285), calls=%async_computation | async-start | bytes 4194304 | tf_op jit(solution)/shard_map/all_to_all | solution.py:106
  37.6 29.8 %copy-start.14 = (bf16[20,20]{1,0:T(8,128)(2,1)S(1)}, bf16[20,20]{1,0:T(8,128)(2,1)}, u32[]{:S(2)}) copy-start(bf16[20,20]{1,0:T(8,128)(2,1)} %param.12) | copy-start | bytes 2404
  67.4 24.3 %copy-start.12 = (bf16[2,24,2,64,1]{3,1,2,0,4:T(8,128)(2,1)S(1)}, bf16[2,24,2,64,1]{3,1,2,0,4:T(8,128)(2,1)}, u32[]{:S(2)}) copy-start(bf16[2,24,2,64,1]{3,1,2,0,4:T(8,128)(2,1)} %constant.67) | copy-start | bytes 36868
  117.9 15.3 %copy-start.5 = (bf16[1,1,20,9216]{3,1,2,0:T(2,128)(2,1)S(1)}, bf16[1,1,20,9216]{3,1,2,0:T(2,128)(2,1)}, u32[]{:S(2)}) copy-start(bf16[1,1,20,9216]{3,1,2,0:T(2,128)(2,1)} %get-tuple-element.45) | copy-start | bytes 1105924
  129.1 53.1 %all-to-all-start.4 = ((bf16[4,2,46080]{2,1,0:T(2,128)(2,1)}), bf16[4,2,46080]{2,1,0:T(2,128)(2,1)S(1)}, u32[]{:S(2)}, u32[]{:S(2)}) async-start(bf16[4,2,46080]{2,1,0:T(2,128)(2,1)} %reshape.393), calls=%async_computation.4 | async-start | bytes 1474560 | tf_op jit(solution)/shard_map/all_to_all | solution.py:135
  170.7 5.6 copy-start.10
  182.2 9.6 %copy-start.4 = (bf16[4,2,46080]{2,1,0:T(2,128)(2,1)}, bf16[4,2,46080]{2,1,0:T(2,128)(2,1)S(1)}, u32[]{:S(2)}) copy-start(bf16[4,2,46080]{2,1,0:T(2,128)(2,1)S(1)} %all-to-all-done.4) | copy-start | bytes 2211844
  182.2 92.4 %all-to-all-start.1 = ((bf16[1,16,64,960]{3,1,0,2:T(8,128)(2,1)}), bf16[1,16,64,960]{3,1,0,2:T(8,128)(2,1)}, u32[]{:S(2)}, u32[]{:S(2)}) async-start(bf16[1,16,64,960]{3,1,0,2:T(8,128)(2,1)} %reshape.388), calls=%async_computation.1 | async-start | bytes 4194304 | tf_op jit(solution)/shard_map/all_to_all | solution.py:117
  210.4 16.4 %copy-start.15 = (bf16[20]{0:T(256)(128)(2,1)S(1)}, bf16[20]{0:T(256)(128)(2,1)}, u32[]{:S(2)}) copy-start(bf16[20]{0:T(256)(128)(2,1)} %param.13) | copy-start | bytes 124
  274.6 8.5 %copy-start.1 = (bf16[1280,960,1]{0,1,2:T(8,128)(2,1)S(1)}, bf16[1280,960,1]{0,1,2:T(8,128)(2,1)}, u32[]{:S(2)}) copy-start(bf16[1280,960,1]{0,1,2:T(8,128)(2,1)} %constant.64) | copy-start | bytes 7372804
  274.6 8.5 %copy-start.9 = (bf16[128,512,1]{1,0,2:T(8,128)(2,1)S(1)}, bf16[128,512,1]{1,0,2:T(8,128)(2,1)}, u32[]{:S(2)}) copy-start(bf16[128,512,1]{1,0,2:T(8,128)(2,1)} %constant.70) | copy-start | bytes 393220
  283.0 11.6 %copy-start.16 = (bf16[128,512,1]{1,0,2:T(8,128)(2,1)S(1)}, bf16[128,512,1]{1,0,2:T(8,128)(2,1)}, u32[]{:S(2)}) copy-start(bf16[128,512,1]{1,0,2:T(8,128)(2,1)} %constant.71) | copy-start | bytes 393220
  351.7 54.1 %all-to-all-start.2 = ((bf16[1,128,8,960]{3,2,0,1:T(8,128)(2,1)}), bf16[1,128,8,960]{3,2,0,1:T(8,128)(2,1)S(1)}, u32[]{:S(2)}, u32[]{:S(2)}) async-start(bf16[1,128,8,960]{3,2,0,1:T(8,128)(2,1)} %copy.306), calls=%async_computation.2 | async-start | bytes 4194304 | tf_op jit(solution)/shard_map/all_to_all | solution.py:106
  380.8 30.2 %copy-start.13 = (bf16[2,24,2,64,1]{3,1,2,0,4:T(8,128)(2,1)S(1)}, bf16[2,24,2,64,1]{3,1,2,0,4:T(8,128)(2,1)}, u32[]{:S(2)}) copy-start(bf16[2,24,2,64,1]{3,1,2,0,4:T(8,128)(2,1)} %constant.67) | copy-start | bytes 36868
  416.1 5.4 slice-start
  416.1 5.4 slice-start.1
  470.8 6.5 %copy-start.3 = (bf16[1,1,20,16,24,24]{5,4,3,2,1,0:T(8,128)(2,1)S(1)}, bf16[1,1,20,16,24,24]{5,4,3,2,1,0:T(8,128)(2,1)}, u32[]{:S(2)}) copy-start(bf16[1,1,20,16,24,24]{5,4,3,2,1,0:T(8,128)(2,1)} %stack.38) | copy-start | bytes 1105924
  472.6 28.3 %collective-permute-start.2 = (bf16[1,2,20,2304]{3,1,2,0:T(2,128)(2,1)S(1)}, bf16[1,2,20,2304]{3,1,2,0:T(2,128)(2,1)S(1)}, u32[]{:S(2)}, u32[]{:S(2)}) collective-permute-start(bf16[1,2,20,2304]{3,1,2,0:T(2,128)(2,1)S(1)} %bitcast.328), channel_id=1, source_target_pairs={{0,24},{8,16},{16,8},{24,0},{1,25},{9,17},{17,9},{25,1},{2,26},{10... | collective-permute-start | bytes 552968 | tf_op jit(solution)/shard_map/ppermute | solution.py:143
  475.7 25.1 %collective-permute-start.1 = (bf16[1,2,20,2304]{3,1,2,0:T(2,128)(2,1)S(1)}, bf16[1,2,20,2304]{3,1,2,0:T(2,128)(2,1)S(1)}, u32[]{:S(2)}, u32[]{:S(2)}) collective-permute-start(bf16[1,2,20,2304]{3,1,2,0:T(2,128)(2,1)S(1)} %bitcast.329), channel_id=1, source_target_pairs={{0,16},{8,24},{16,0},{24,8},{1,17},{9,25},{17,1},{25,9},{2,18},{10... | collective-permute-start | bytes 552968 | tf_op jit(solution)/shard_map/ppermute | solution.py:143
  477.2 23.6 %collective-permute-start = (bf16[1,2,20,2304]{3,1,2,0:T(2,128)(2,1)}, bf16[1,2,20,2304]{3,1,2,0:T(2,128)(2,1)S(1)}, u32[]{:S(2)}, u32[]{:S(2)}) collective-permute-start(bf16[1,2,20,2304]{3,1,2,0:T(2,128)(2,1)} %bitcast.307), channel_id=1, source_target_pairs={{0,8},{8,0},{16,24},{24,16},{1,9},{9,1},{17,25},{25,17},{2,10},{10... | collective-permute-start | bytes 552968 | tf_op jit(solution)/shard_map/ppermute | solution.py:143
  484.6 5.7 copy-start.11
  496.3 73.1 %all-to-all-start.3 = ((bf16[1,16,64,960]{3,1,0,2:T(8,128)(2,1)}), bf16[1,16,64,960]{3,1,0,2:T(8,128)(2,1)}, u32[]{:S(2)}, u32[]{:S(2)}) async-start(bf16[1,16,64,960]{3,1,0,2:T(8,128)(2,1)} %reshape.391), calls=%async_computation.3 | async-start | bytes 4194304 | tf_op jit(solution)/shard_map/all_to_all | solution.py:117
  550.7 2.3 copy-start
  569.3 7.5 %copy-start.8 = (bf16[128,512,1]{1,0,2:T(8,128)(2,1)S(1)}, bf16[128,512,1]{1,0,2:T(8,128)(2,1)}, u32[]{:S(2)}) copy-start(bf16[128,512,1]{1,0,2:T(8,128)(2,1)} %constant.63) | copy-start | bytes 393220
  576.8 13.4 %copy-start.7 = (bf16[128,512,1]{1,0,2:T(8,128)(2,1)S(1)}, bf16[128,512,1]{1,0,2:T(8,128)(2,1)}, u32[]{:S(2)}) copy-start(bf16[128,512,1]{1,0,2:T(8,128)(2,1)} %constant.65) | copy-start | bytes 393220
